TPU v7x, 256 devices: a whole 4x4x8 slice. The times are simulated.
256 devices in a mesh: blk: 128 (over z, y, x), chan: 2 (over core).
Axes of the slice: x: 4, y: 4, z: 8, core: 2. Of those that a mesh axis runs over, the one named last changes fastest.
Arguments:
- inputs: bfloat16 [128, 512, 512], P('chan', 'blk'), may hold values from -6 to 6
- w_first: bfloat16 [3, 3, 128, 128], P(None, None, 'chan'), may hold values from -0.1875 to 0.1875
- w_second: bfloat16 [3, 3, 128, 128], P(None, None, 'chan'), may hold values from -0.1875 to 0.1875
- w_third: bfloat16 [3, 3, 256, 128], P(None, None, 'chan'), may hold values from -0.1875 to 0.1875
- cotangent: bfloat16 [256, 256, 256], P('chan', 'blk'), may hold values from -6 to 6
- mirror: int32 [128], P('blk'), may hold values from 0 to 1
Outputs:
- grad_inputs: bfloat16 [128, 512, 512], P('chan', 'blk')
- grad_first: float32 [3, 3, 128, 128], P(None, None, 'chan')
- grad_second: float32 [3, 3, 128, 128], P(None, None, 'chan')
- grad_third: float32 [3, 3, 256, 128], P(None, None, 'chan')
Inputs may be any that keep to these rules, and one draw needn't show every extreme that they name: `mirror`: 1 marks a tile whose columns are stored in reverse order, 0 a tile stored in the cycle's order.
All inputs are finite; a program needn't handle non-finite values.
Results may differ from a plain program's by a relative error of at most 0.024.
Values may be sent and summed in bfloat16 or wider, within the bound.
A program may use at most 64 MiB of HBM per device.

v0:
```python
import math
import jax
import jax.numpy as jnp
from jax import lax
from jax.sharding import PartitionSpec as P


def extended(shard, sides, width):
    for axis, dim in sides:
        devices, length = (lax.axis_size(axis), shard.shape[dim])
        up = [(i, (i + 1) % devices) for i in range(devices)]
        down = [(j, i) for i, j in up]
        last = lax.slice_in_dim(shard, length - width, length, axis=dim)
        leading = lax.slice_in_dim(shard, 0, width, axis=dim)
        before = lax.ppermute(last, axis, up)
        after = lax.ppermute(leading, axis, down)
        shard = jnp.concatenate([before, shard, after], axis=dim)
    return shard


def passed_along(shard, axis, by):
    devices = lax.axis_size(axis)
    return lax.ppermute(shard, axis, [(i, (i + by) % devices) for i in range(devices)])


def orient(block, mirrored):
    return jnp.where(mirrored == 1, block[..., ::-1], block)


def widen(active):
    gathered = lax.all_gather(active, "chan", axis=0, tiled=True)
    return extended(gathered, (("blk", 1),), 1)


def widen_by(active, before_rows, after_rows):
    gathered = lax.all_gather(active, "chan", axis=0, tiled=True)
    devices, length = (lax.axis_size("blk"), gathered.shape[1])
    up = [(i, (i + 1) % devices) for i in range(devices)]
    down = [(j, i) for i, j in up]
    before = lax.ppermute(gathered[:, length - before_rows :], "blk", up)
    after = lax.ppermute(gathered[:, :after_rows], "blk", down)
    return jnp.concatenate([before, gathered, after], axis=1)


def conv_taps(padded, weight):
    row_count = padded.shape[1] - 2
    col_count = padded.shape[2]
    framed = jnp.pad(padded, ((0, 0), (0, 0), (1, 1)))
    running = jnp.zeros((weight.shape[2], row_count, col_count), jnp.float32)
    for row_tap in range(3):
        for col_tap in range(3):
            running = running + jnp.einsum(
                "oi,irw->orw",
                weight[row_tap, col_tap],
                framed[:, row_tap : row_tap + row_count, col_tap : col_tap + col_count],
                preferred_element_type=jnp.float32,
            )
    return running


def weight_taps(grad_out, padded):
    row_count = grad_out.shape[1]
    col_count = grad_out.shape[2]
    framed = jnp.pad(padded, ((0, 0), (0, 0), (1, 1)))
    views = jnp.stack(
        [
            framed[:, row_tap : row_tap + row_count, col_tap : col_tap + col_count]
            for row_tap in range(3)
            for col_tap in range(3)
        ]
    )
    taps = jnp.einsum("orw,kirw->koi", grad_out, views, preferred_element_type=jnp.float32)
    return taps.reshape((3, 3) + taps.shape[1:])


def spread_taps(grad_out, weight):
    row_count = grad_out.shape[1]
    col_count = grad_out.shape[2]
    framed = jnp.pad(grad_out, ((0, 0), (2, 2), (2, 2)))
    running = jnp.zeros((weight.shape[3], row_count + 2, col_count), jnp.float32)
    for row_tap in range(3):
        for col_tap in range(3):
            row_start = 2 - row_tap
            col_start = 3 - col_tap
            running = running + jnp.einsum(
                "oi,orw->irw",
                weight[row_tap, col_tap],
                framed[:, row_start : row_start + row_count + 2, col_start : col_start + col_count],
                preferred_element_type=jnp.float32,
            )
    return running


def spread_stride(grad_out, weight):
    out_rows = grad_out.shape[1]
    out_cols = grad_out.shape[2]
    channels = weight.shape[3]
    framed = jnp.pad(grad_out, ((0, 0), (1, 1), (1, 1)))
    parity_rows = []
    for row_par in range(2):
        parity_cols = []
        for col_par in range(2):
            running = jnp.zeros((channels, out_rows + 1, out_cols + 1), jnp.float32)
            for row_tap in range(row_par, 3, 2):
                for col_tap in range(col_par, 3, 2):
                    row_start = 1 - row_tap // 2
                    col_start = 1 - col_tap // 2
                    running = running + jnp.einsum(
                        "oi,orw->irw",
                        weight[row_tap, col_tap],
                        framed[
                            :,
                            row_start : row_start + out_rows + 1,
                            col_start : col_start + out_cols + 1,
                        ],
                        preferred_element_type=jnp.float32,
                    )
            parity_cols.append(running)
        parity_rows.append(jnp.stack(parity_cols, axis=3))
    woven = jnp.stack(parity_rows, axis=2)
    woven = woven.reshape(channels, 2 * out_rows + 2, 2 * out_cols + 2)
    return woven[:, : 2 * out_rows + 1, 1 : 2 * out_cols + 1]


def fold_rims(grad_rows, both_sides):
    interior = grad_rows[:, 1:-1] if both_sides else grad_rows[:, 1:]
    from_next = passed_along(grad_rows[:, :1].astype(jnp.bfloat16), "blk", -1).astype(jnp.float32)
    if both_sides:
        from_prev = passed_along(grad_rows[:, -1:].astype(jnp.bfloat16), "blk", 1).astype(
            jnp.float32
        )
        return jnp.concatenate(
            [interior[:, :1] + from_prev, interior[:, 1:-1], interior[:, -1:] + from_next], axis=1
        )
    return jnp.concatenate([interior[:, :-1], interior[:, -1:] + from_next], axis=1)


def own_inputs(weight):
    whole = lax.all_gather(weight, "chan", axis=2, tiled=True)
    width = whole.shape[3] // lax.axis_size("chan")
    return lax.dynamic_slice_in_dim(whole, lax.axis_index("chan") * width, width, axis=3)


def input_grad(delta, weight):
    every = lax.all_gather(delta, "chan", axis=0, tiled=True)
    return fold_rims(spread_taps(every, weight), True)


def third_input_grad(upstream, weight):
    every = lax.all_gather(upstream, "chan", axis=0, tiled=True)
    return fold_rims(spread_stride(every, weight), False)


def parity_picker(cols, out_cols):
    source = lax.broadcasted_iota(jnp.int32, (cols, 3 * out_cols), 0)
    target = lax.broadcasted_iota(jnp.int32, (cols, 3 * out_cols), 1)
    wanted = 2 * (target % out_cols) + target // out_cols - 1
    return (source == wanted).astype(jnp.bfloat16)


def summed_over_cycle(parts, axis):
    devices = lax.axis_size(axis)
    flat = jnp.concatenate([p.reshape(-1) for p in parts])
    pieces = lax.all_to_all(flat.reshape(devices, -1), axis, 0, 0, tiled=True)
    total = jnp.sum(pieces, axis=0)
    spread = jnp.broadcast_to(total[None], (devices,) + total.shape)
    whole = lax.all_to_all(spread, axis, 0, 0, tiled=True).reshape(-1)
    out, start = ([], 0)
    for p in parts:
        out.append(whole[start : start + p.size].reshape(p.shape))
        start += p.size
    return out


def gelu_back(pre_act, grad_in):
    return jax.vjp(jax.nn.gelu, pre_act)[1](grad_in)[0]


def shards(inputs, w_first, w_second, w_third, cotangent, mirror):
    mirrored = mirror[0]
    oriented = orient(inputs, mirrored)
    upstream = orient(cotangent, mirrored)
    first_wide = widen_by(oriented, 3, 2)
    first_pre_wide = conv_taps(first_wide, w_first)
    first_act_wide = jax.nn.gelu(first_pre_wide).astype(jnp.bfloat16)
    first_pad = first_wide[:, 2:-1]
    first_pre = first_pre_wide[:, 2:-1]
    second_wide = lax.all_gather(first_act_wide, "chan", axis=0, tiled=True)
    second_pre_wide = conv_taps(second_wide, w_second)
    second_act_wide = jax.nn.gelu(second_pre_wide).astype(jnp.bfloat16)
    second_pad = second_wide[:, 1:]
    second_pre = second_pre_wide[:, 1:]
    stride_rows = lax.all_gather(second_act_wide, "chan", axis=0, tiled=True)
    out_rows = upstream.shape[1]
    out_cols = upstream.shape[2]
    by_parity = jnp.einsum(
        "irt,tk->irk",
        stride_rows,
        parity_picker(2 * out_cols, out_cols),
        preferred_element_type=jnp.float32,
    ).astype(jnp.bfloat16)
    spaced = jnp.stack([upstream, jnp.zeros_like(upstream)], axis=2).reshape(
        upstream.shape[0], 2 * out_rows, out_cols
    )
    row_placed = jnp.stack(
        [
            jnp.pad(spaced, ((0, 0), (row_tap, 1), (0, 0)))[:, : 2 * out_rows + 1]
            for row_tap in range(3)
        ]
    )
    third_grad = jnp.stack(
        [
            jnp.einsum(
                "aosc,isc->aoi",
                row_placed,
                by_parity[:, :, col_tap * out_cols : (col_tap + 1) * out_cols],
                preferred_element_type=jnp.float32,
            )
            for col_tap in range(3)
        ],
        axis=1,
    )
    second_back = third_input_grad(upstream, own_inputs(w_third))
    second_delta = gelu_back(second_pre, second_back).astype(jnp.bfloat16)
    second_grad = weight_taps(second_delta, second_pad)
    first_back = input_grad(second_delta, own_inputs(w_second))
    first_delta = gelu_back(first_pre, first_back).astype(jnp.bfloat16)
    first_grad = weight_taps(first_delta, first_pad)
    input_back = input_grad(first_delta, own_inputs(w_first)).astype(jnp.bfloat16)
    reduced = summed_over_cycle((first_grad, second_grad, third_grad), "blk")
    cell_count = inputs.shape[1] * inputs.shape[2] * lax.axis_size("blk")
    return (
        orient(input_back, mirrored),
        reduced[0] / math.sqrt(cell_count),
        reduced[1] / math.sqrt(cell_count),
        reduced[2] / math.sqrt(cell_count // 4),
    )


def solution(mesh):
    placed = (
        P("chan", "blk", None),
        P(None, None, "chan", None),
        P(None, None, "chan", None),
        P(None, None, "chan", None),
        P("chan", "blk", None),
        P("blk"),
    )
    return jax.shard_map(
        shards,
        mesh=mesh,
        in_specs=placed,
        out_specs=(
            P("chan", "blk", None),
            P(None, None, "chan", None),
            P(None, None, "chan", None),
            P(None, None, "chan", None),
        ),
        check_vma=False,
    )
```

profile of v0, /device:TPU:8, one launch (start us, length us, event | category | flops | bytes accessed | tf_op | source)
XLA Modules:
  0.0 161.4 jit_solution(18438336296300883969)
XLA Ops:
  3.9 2.3 %all_gather.31 = bf16[128,4,512]{2,0,1:T(8,128)(2,1)S(1)} all-gather(bf16[64,4,512]{2,0,1:T(8,128)(2,1)S(1)} %broadcast_select_fusion.1), channel_id=1, replica_groups=mesh['blk'=128,'chan'=2] {'chan'}, dimensions={0}, use_global_device_ids=true | all-gather | bytes 786432 | tf_op jit(solution)/shard_map/all_gather | solution.py:36
  7.0 1.5 collective-permute-start.1
  9.2 2.6 %collective-permute-start.2 = (bf16[128,2,512]{2,0,1:T(8,128)(2,1)}, bf16[128,2,512]{2,0,1:T(8,128)(2,1)}, u32[]{:S(2)}, u32[]{:S(2)}) collective-permute-start(bf16[128,2,512]{2,0,1:T(8,128)(2,1)} %slice.570), channel_id=1, source_target_pairs={{2,0},{4,2},{6,4},{8,6},{10,8},{12,10},{14,12},{16,14},{18,16},{20... | collective-permute-start | bytes 786440 | tf_op jit(solution)/shard_map/ppermute | solution.py:41
  12.2 2.0 %all_gather.30 = bf16[256,2,256]{0,2,1:T(8,128)(2,1)S(1)} all-gather(bf16[128,2,256]{0,2,1:T(8,128)(2,1)S(1)} %broadcast_select_fusion.2), channel_id=1, replica_groups=mesh['blk'=128,'chan'=2] {'chan'}, dimensions={0}, use_global_device_ids=true | all-gather | bytes 393216 | tf_op jit(solution)/shard_map/all_gather | solution.py:150
  14.4 2.2 %all_gather.29 = bf16[3,3,256,128]{2,3,1,0:T(8,128)(2,1)S(1)} all-gather(bf16[3,3,128,128]{2,3,1,0:T(8,128)(2,1)S(1)} %copy.62), channel_id=1, replica_groups=mesh['blk'=128,'chan'=2] {'chan'}, dimensions={2}, use_global_device_ids=true | all-gather | bytes 884736 | tf_op jit(solution)/shard_map/all_gather | solution.py:139
  20.1 2.3 %reshape.51 = f32[64,6,514]{0,2,1:T(8,128)} reshape(f32[64,3,2,257,2]{0,4,3,2,1:T(2,128)S(1)} %copy.65) | data formatting | bytes 1579008 | tf_op jit(solution)/shard_map/reshape | solution.py:121
  27.2 2.0 %all_gather.28 = bf16[3,3,128,128]{3,2,1,0:T(8,128)(2,1)S(1)} all-gather(bf16[3,3,64,128]{3,2,1,0:T(8,128)(2,1)S(1)} %copy-done), channel_id=1, replica_groups=mesh['blk'=128,'chan'=2] {'chan'}, dimensions={2}, use_global_device_ids=true | all-gather | bytes 442368 | tf_op jit(solution)/shard_map/all_gather | solution.py:139
  35.5 2.6 %all_gather.32 = bf16[128,7,512]{2,0,1:T(8,128)(2,1)S(1)} all-gather(bf16[64,7,512]{2,0,1:T(8,128)(2,1)S(1)} %get-tuple-element.41), channel_id=1, replica_groups=mesh['blk'=128,'chan'=2] {'chan'}, dimensions={0}, use_global_device_ids=true | all-gather | bytes 1376256 | tf_op jit(solution)/shard_map/all_gather | solution.py:188
  41.5 2.3 %all_gather.35 = bf16[128,5,512]{2,0,1:T(8,128)(2,1)S(1)} all-gather(bf16[64,5,512]{2,0,1:T(8,128)(2,1)S(1)} %get-tuple-element.47), channel_id=1, replica_groups=mesh['blk'=128,'chan'=2] {'chan'}, dimensions={0}, use_global_device_ids=true | all-gather | bytes 983040 | tf_op jit(solution)/shard_map/all_gather | solution.py:193
  47.6 2.2 %all_gather.33 = bf16[128,4,512]{2,0,1:T(8,128)(2,1)S(1)} all-gather(bf16[64,4,512]{2,0,1:T(8,128)(2,1)S(1)} %fusion.63), channel_id=1, replica_groups=mesh['blk'=128,'chan'=2] {'chan'}, dimensions={0}, use_global_device_ids=true | all-gather | bytes 786432 | tf_op jit(solution)/shard_map/all_gather | solution.py:145
  53.4 1.6 collective-permute-start.3
  55.0 2.6 %collective-permute-start.4 = (bf16[64,1,512]{2,0,1:T(8,128)(2,1)S(1)}, bf16[64,1,512]{2,0,1:T(8,128)(2,1)S(1)}, u32[]{:S(2)}, u32[]{:S(2)}) collective-permute-start(bf16[64,1,512]{2,0,1:T(8,128)(2,1)S(1)} %get-tuple-element.35), channel_id=1, source_target_pairs={{0,254},{2,0},{4,2},{6,4},{8,6},{10,8},{12,10},{14,12},{16,14},{18... | collective-permute-start | bytes 196616 | tf_op jit(solution)/shard_map/ppermute | solution.py:23
  59.4 1.5 fusion.103
  62.7 1.5 fusion.105
  65.4 19.3 %all-to-all-start = ((f32[128,1,2304]{2,1,0:T(1,128)}), f32[128,1,2304]{2,1,0:T(1,128)S(1)}, u32[]{:S(2)}, u32[]{:S(2)}) async-start(f32[128,1,2304]{2,1,0:T(1,128)} %bitcast.146), calls=%async_computation | async-start | bytes 2359296 | tf_op jit(solution)/shard_map/all_to_all | solution.py:164
  84.7 2.0 %all_gather.27 = bf16[3,3,128,128]{3,2,1,0:T(8,128)(2,1)S(1)} all-gather(bf16[3,3,64,128]{3,2,1,0:T(8,128)(2,1)S(1)} %copy-done.1), channel_id=1, replica_groups=mesh['blk'=128,'chan'=2] {'chan'}, dimensions={2}, use_global_device_ids=true | all-gather | bytes 442368 | tf_op jit(solution)/shard_map/all_gather | solution.py:139
  86.7 2.2 %all_gather.34 = bf16[128,4,512]{2,0,1:T(8,128)(2,1)S(1)} all-gather(bf16[64,4,512]{2,0,1:T(8,128)(2,1)S(1)} %fusion.70), channel_id=1, replica_groups=mesh['blk'=128,'chan'=2] {'chan'}, dimensions={0}, use_global_device_ids=true | all-gather | bytes 786432 | tf_op jit(solution)/shard_map/all_gather | solution.py:145
  90.1 27.3 %all-to-all-done = f32[128,1,2304]{2,1,0:T(1,128)S(1)} async-done(((f32[128,1,2304]{2,1,0:T(1,128)}), f32[128,1,2304]{2,1,0:T(1,128)S(1)}, u32[]{:S(2)}, u32[]{:S(2)}) %all-to-all-start) | async-done | bytes 1179680 | tf_op jit(solution)/shard_map/all_to_all | solution.py:164
  118.1 1.7 %broadcast_in_dim.2 = f32[128,1,2304]{2,1,0:T(1,128)} broadcast(f32[2304]{0:T(1024)S(1)} %reduce_sum.9), dimensions={2} | broadcast | bytes 1188864 | tf_op jit(solution)/shard_map/broadcast_in_dim | solution.py:166
  119.7 6.3 %all-to-all-start.1 = ((f32[128,1,2304]{2,1,0:T(1,128)}), f32[128,1,2304]{2,1,0:T(1,128)S(1)}, u32[]{:S(2)}, u32[]{:S(2)}) async-start(f32[128,1,2304]{2,1,0:T(1,128)} %broadcast_in_dim.2), calls=%async_computation.1 | async-start | bytes 2359296 | tf_op jit(solution)/shard_map/all_to_all | solution.py:167
  128.5 1.8 %collective-permute-start.5 = (bf16[64,1,512]{2,0,1:T(8,128)(2,1)S(1)}, bf16[64,1,512]{2,0,1:T(8,128)(2,1)S(1)}, u32[]{:S(2)}, u32[]{:S(2)}) collective-permute-start(bf16[64,1,512]{2,0,1:T(8,128)(2,1)S(1)} %get-tuple-element.32), channel_id=1, source_target_pairs={{0,2},{2,4},{4,6},{6,8},{8,10},{10,12},{12,14},{14,16},{16,18},{18... | collective-permute-start | bytes 196616 | tf_op jit(solution)/shard_map/ppermute | solution.py:23
  130.3 2.7 %collective-permute-start.6 = (bf16[64,1,512]{2,0,1:T(8,128)(2,1)S(1)}, bf16[64,1,512]{2,0,1:T(8,128)(2,1)S(1)}, u32[]{:S(2)}, u32[]{:S(2)}) collective-permute-start(bf16[64,1,512]{2,0,1:T(8,128)(2,1)S(1)} %get-tuple-element.33), channel_id=1, source_target_pairs={{0,254},{2,0},{4,2},{6,4},{8,6},{10,8},{12,10},{14,12},{16,14},{18... | collective-permute-start | bytes 196616 | tf_op jit(solution)/shard_map/ppermute | solution.py:23
  133.0 3.0 %collective-permute-done.5 = bf16[64,1,512]{2,0,1:T(8,128)(2,1)S(1)} collective-permute-done((bf16[64,1,512]{2,0,1:T(8,128)(2,1)S(1)}, bf16[64,1,512]{2,0,1:T(8,128)(2,1)S(1)}, u32[]{:S(2)}, u32[]{:S(2)}) %collective-permute-start.5) | collective-permute-done | bytes 65568 | tf_op jit(solution)/shard_map/ppermute | solution.py:23
  137.5 21.2 %all-to-all-done.1 = f32[128,1,2304]{2,1,0:T(1,128)S(1)} async-done(((f32[128,1,2304]{2,1,0:T(1,128)}), f32[128,1,2304]{2,1,0:T(1,128)S(1)}, u32[]{:S(2)}, u32[]{:S(2)}) %all-to-all-start.1) | async-done | bytes 1179680 | tf_op jit(solution)/shard_map/all_to_all | solution.py:167
  (130 shorter events, 42.6 us)
Async XLA Ops:
  2.8 9.0 %copy-start.3 = (bf16[128,2,256]{2,1,0:T(2,128)(2,1)S(1)}, bf16[128,2,256]{2,1,0:T(2,128)(2,1)}, u32[]{:S(2)}) copy-start(bf16[128,2,256]{2,1,0:T(2,128)(2,1)} %param.10) | copy-start | bytes 393220
  3.9 10.3 %copy-start.2 = (bf16[3,3,128,128]{3,2,1,0:T(8,128)(2,1)S(1)}, bf16[3,3,128,128]{3,2,1,0:T(8,128)(2,1)}, u32[]{:S(2)}) copy-start(bf16[3,3,128,128]{3,2,1,0:T(8,128)(2,1)} %param.9) | copy-start | bytes 884740
  7.0 22.3 %collective-permute-start.1 = (bf16[128,3,512]{2,0,1:T(8,128)(2,1)}, bf16[128,3,512]{2,0,1:T(8,128)(2,1)}, u32[]{:S(2)}, u32[]{:S(2)}) collective-permute-start(bf16[128,3,512]{2,0,1:T(8,128)(2,1)} %slice.569), channel_id=1, source_target_pairs={{0,2},{2,4},{4,6},{6,8},{8,10},{10,12},{12,14},{14,16},{16,18},{18... | collective-permute-start | bytes 1179656 | tf_op jit(solution)/shard_map/ppermute | solution.py:40
  9.2 21.3 %collective-permute-start.2 = (bf16[128,2,512]{2,0,1:T(8,128)(2,1)}, bf16[128,2,512]{2,0,1:T(8,128)(2,1)}, u32[]{:S(2)}, u32[]{:S(2)}) collective-permute-start(bf16[128,2,512]{2,0,1:T(8,128)(2,1)} %slice.570), channel_id=1, source_target_pairs={{2,0},{4,2},{6,4},{8,6},{10,8},{12,10},{14,12},{16,14},{18,16},{20... | collective-permute-start | bytes 786440 | tf_op jit(solution)/shard_map/ppermute | solution.py:41
  23.5 5.7 %collective-permute-start = (bf16[64,1,512]{2,0,1:T(8,128)(2,1)S(1)}, bf16[64,1,512]{2,0,1:T(8,128)(2,1)S(1)}, u32[]{:S(2)}, u32[]{:S(2)}) collective-permute-start(bf16[64,1,512]{2,0,1:T(8,128)(2,1)S(1)} %copy.104), channel_id=1, source_target_pairs={{0,254},{2,0},{4,2},{6,4},{8,6},{10,8},{12,10},{14,12},{16,14},{18... | collective-permute-start | bytes 196616 | tf_op jit(solution)/shard_map/ppermute | solution.py:23
  26.3 0.9 copy-start
  30.3 1.2 copy-start.1
  53.4 8.8 %collective-permute-start.3 = (bf16[64,1,512]{2,0,1:T(8,128)(2,1)S(1)}, bf16[64,1,512]{2,0,1:T(8,128)(2,1)S(1)}, u32[]{:S(2)}, u32[]{:S(2)}) collective-permute-start(bf16[64,1,512]{2,0,1:T(8,128)(2,1)S(1)} %get-tuple-element.34), channel_id=1, source_target_pairs={{0,2},{2,4},{4,6},{6,8},{8,10},{10,12},{12,14},{14,16},{16,18},{18... | collective-permute-start | bytes 196616 | tf_op jit(solution)/shard_map/ppermute | solution.py:23
  55.0 7.3 %collective-permute-start.4 = (bf16[64,1,512]{2,0,1:T(8,128)(2,1)S(1)}, bf16[64,1,512]{2,0,1:T(8,128)(2,1)S(1)}, u32[]{:S(2)}, u32[]{:S(2)}) collective-permute-start(bf16[64,1,512]{2,0,1:T(8,128)(2,1)S(1)} %get-tuple-element.35), channel_id=1, source_target_pairs={{0,254},{2,0},{4,2},{6,4},{8,6},{10,8},{12,10},{14,12},{16,14},{18... | collective-permute-start | bytes 196616 | tf_op jit(solution)/shard_map/ppermute | solution.py:23
  65.4 52.0 %all-to-all-start = ((f32[128,1,2304]{2,1,0:T(1,128)}), f32[128,1,2304]{2,1,0:T(1,128)S(1)}, u32[]{:S(2)}, u32[]{:S(2)}) async-start(f32[128,1,2304]{2,1,0:T(1,128)} %bitcast.146), calls=%async_computation | async-start | bytes 2359296 | tf_op jit(solution)/shard_map/all_to_all | solution.py:164
  119.7 39.0 %all-to-all-start.1 = ((f32[128,1,2304]{2,1,0:T(1,128)}), f32[128,1,2304]{2,1,0:T(1,128)S(1)}, u32[]{:S(2)}, u32[]{:S(2)}) async-start(f32[128,1,2304]{2,1,0:T(1,128)} %broadcast_in_dim.2), calls=%async_computation.1 | async-start | bytes 2359296 | tf_op jit(solution)/shard_map/all_to_all | solution.py:167
  128.5 7.5 %collective-permute-start.5 = (bf16[64,1,512]{2,0,1:T(8,128)(2,1)S(1)}, bf16[64,1,512]{2,0,1:T(8,128)(2,1)S(1)}, u32[]{:S(2)}, u32[]{:S(2)}) collective-permute-start(bf16[64,1,512]{2,0,1:T(8,128)(2,1)S(1)} %get-tuple-element.32), channel_id=1, source_target_pairs={{0,2},{2,4},{4,6},{6,8},{8,10},{10,12},{12,14},{14,16},{16,18},{18... | collective-permute-start | bytes 196616 | tf_op jit(solution)/shard_map/ppermute | solution.py:23
  130.3 5.7 %collective-permute-start.6 = (bf16[64,1,512]{2,0,1:T(8,128)(2,1)S(1)}, bf16[64,1,512]{2,0,1:T(8,128)(2,1)S(1)}, u32[]{:S(2)}, u32[]{:S(2)}) collective-permute-start(bf16[64,1,512]{2,0,1:T(8,128)(2,1)S(1)} %get-tuple-element.33), channel_id=1, source_target_pairs={{0,254},{2,0},{4,2},{6,4},{8,6},{10,8},{12,10},{14,12},{16,14},{18... | collective-permute-start | bytes 196616 | tf_op jit(solution)/shard_map/ppermute | solution.py:23
where the time goes:
time: 162 us; the launch traced here: 161 us
  waiting for transfers between devices  51.5 us (32%)
  starting transfers between devices  39.1 us (24%)
  matrix products  21.5 us (13%)
  local copies, waits for them, and re-layouts  19.8 us (12%)
  blocking collectives  19.8 us (12%)
  other arithmetic  7.65 us (5%)
  between operations  2.11 us (1%)
    all_to_all x1, waiting for transfers between devices, summed_over_cycle(): pieces = lax.all_to_all(flat.reshape(devices, -1), axis, 0, 0, tiled=True)  27.3 us
    all_to_all x1, waiting for transfers between devices, summed_over_cycle(): whole = lax.all_to_all(spread, axis, 0, 0, tiled=True).reshape(-1)  21.2 us
    all_to_all x1, starting transfers between devices, summed_over_cycle(): pieces = lax.all_to_all(flat.reshape(devices, -1), axis, 0, 0, tiled=True)  19.3 us
    ppermute x5, starting transfers between devices, passed_along(): lax.ppermute(shard, axis, [(i, (i + by) % devices) for i in range(devices)])  9.3 us
    dot_general x18, matrix products, conv_taps(): jnp.einsum('oi,irw->orw', weight[row_tap, col_tap], framed[:, row_tap:row...  7.17 us
    dot_general x18, matrix products, spread_taps(): jnp.einsum('oi,orw->irw', weight[row_tap, col_tap], framed[:, row_start:r...  7.11 us
    unnamed x32, local copies, waits for them, and re-layouts  7.02 us
    all_to_all x1, starting transfers between devices, summed_over_cycle(): whole = lax.all_to_all(spread, axis, 0, 0, tiled=True).reshape(-1)  6.34 us
  transfers between devices with their start and end apart: 9, of which 3 were waited for; matrix products, arithmetic and copies ran while one was open for 13% of the time, Pallas kernels for 0%

commit v1 on v0

--- a/solution.py
+++ b/solution.py
@@ -3,6 +3,13 @@
 import jax.numpy as jnp
 from jax import lax
 from jax.sharding import PartitionSpec as P
+
+
+def all_by_exchange(x, mesh_axis, dim):
+    size = lax.axis_size(mesh_axis)
+    shards = jnp.stack([x for _ in range(size)])
+    shards = lax.all_to_all(shards, mesh_axis, split_axis=0, concat_axis=0)
+    return jnp.concatenate(shards, axis=dim)
 
 
 def extended(shard, sides, width):
@@ -142,7 +149,7 @@
 
 
 def input_grad(delta, weight):
-    every = lax.all_gather(delta, "chan", axis=0, tiled=True)
+    every = all_by_exchange(delta, "chan", 0)
     return fold_rims(spread_taps(every, weight), True)
 
 

time: 162 us -> 171 us (1.056)
  waiting for transfers between devices: 51.5 us -> 56.3 us
  starting transfers between devices: 39.1 us -> 42.5 us
    all_gather x2 -> x0, blocking collectives: 4.35 us -> none  [input_grad(): every = lax.all_gather(delta, 'chan', axis=0, tiled=True)]
    all_to_all x0 -> x1, blocking collectives: none -> 4.15 us  [all_by_exchange(): shards = lax.all_to_all(shards, mesh_axis, split_axis=0, concat_axis=0)]
    all_to_all x1, waiting for transfers between devices: 27.3 us -> 30.9 us  [summed_over_cycle(): pieces = lax.all_to_all(flat.reshape(devices, -1), axis, 0, 0, tiled=True)]
    all_to_all x0 -> x1, starting transfers between devices: none -> 3.49 us  [all_by_exchange(): shards = lax.all_to_all(shards, mesh_axis, split_axis=0, concat_axis=0)]
  transfers between devices with their start and end apart: 9 -> 10, of which waited for: 3 -> 4; matrix products, arithmetic and copies ran while one was open for 13% -> 13% of each run, Pallas kernels for 0% -> 0%
where the time goes in v1:
time: 171 us; the launch traced here: 170 us
  waiting for transfers between devices  56.3 us (33%)
  starting transfers between devices  42.5 us (25%)
  matrix products  21.5 us (13%)
  local copies, waits for them, and re-layouts  19.8 us (12%)
  blocking collectives  19.6 us (11%)
  other arithmetic  8.49 us (5%)
  between operations  2.13 us (1%)
    all_to_all x1, waiting for transfers between devices, summed_over_cycle(): pieces = lax.all_to_all(flat.reshape(devices, -1), axis, 0, 0, tiled=True)  30.9 us
    all_to_all x1, waiting for transfers between devices, summed_over_cycle(): whole = lax.all_to_all(spread, axis, 0, 0, tiled=True).reshape(-1)  21.3 us
    all_to_all x1, starting transfers between devices, summed_over_cycle(): pieces = lax.all_to_all(flat.reshape(devices, -1), axis, 0, 0, tiled=True)  19.3 us
    ppermute x5, starting transfers between devices, passed_along(): lax.ppermute(shard, axis, [(i, (i + by) % devices) for i in range(devices)])  9.3 us
    dot_general x18, matrix products, conv_taps(): jnp.einsum('oi,irw->orw', weight[row_tap, col_tap], framed[:, row_tap:row...  7.17 us
    dot_general x18, matrix products, spread_taps(): jnp.einsum('oi,orw->irw', weight[row_tap, col_tap], framed[:, row_start:r...  7.12 us
    unnamed x32, local copies, waits for them, and re-layouts  7.02 us
    all_to_all x1, starting transfers between devices, summed_over_cycle(): whole = lax.all_to_all(spread, axis, 0, 0, tiled=True).reshape(-1)  6.34 us
  transfers between devices with their start and end apart: 10, of which 4 were waited for; matrix products, arithmetic and copies ran while one was open for 13% of the time, Pallas kernels for 0%

profile of v1, /device:TPU:8, one launch (start us, length us, event | category | flops | bytes accessed | tf_op | source)
XLA Modules:
  0.0 170.4 jit_solution(7247264507438603536)
XLA Ops:
  3.9 2.3 %all_gather.25 = bf16[128,4,512]{2,0,1:T(8,128)(2,1)S(1)} all-gather(bf16[64,4,512]{2,0,1:T(8,128)(2,1)S(1)} %broadcast_select_fusion.1), channel_id=1, replica_groups=mesh['blk'=128,'chan'=2] {'chan'}, dimensions={0}, use_global_device_ids=true | all-gather | bytes 786432 | tf_op jit(solution)/shard_map/all_gather | solution.py:43
  7.0 1.5 collective-permute-start.1
  9.2 2.6 %collective-permute-start.2 = (bf16[128,2,512]{2,0,1:T(8,128)(2,1)}, bf16[128,2,512]{2,0,1:T(8,128)(2,1)}, u32[]{:S(2)}, u32[]{:S(2)}) collective-permute-start(bf16[128,2,512]{2,0,1:T(8,128)(2,1)} %slice.570), channel_id=1, source_target_pairs={{2,0},{4,2},{6,4},{8,6},{10,8},{12,10},{14,12},{16,14},{18,16},{20... | collective-permute-start | bytes 786440 | tf_op jit(solution)/shard_map/ppermute | solution.py:48
  12.2 2.0 %all_gather.24 = bf16[256,2,256]{0,2,1:T(8,128)(2,1)S(1)} all-gather(bf16[128,2,256]{0,2,1:T(8,128)(2,1)S(1)} %broadcast_select_fusion.2), channel_id=1, replica_groups=mesh['blk'=128,'chan'=2] {'chan'}, dimensions={0}, use_global_device_ids=true | all-gather | bytes 393216 | tf_op jit(solution)/shard_map/all_gather | solution.py:157
  14.4 2.2 %all_gather.23 = bf16[3,3,256,128]{2,3,1,0:T(8,128)(2,1)S(1)} all-gather(bf16[3,3,128,128]{2,3,1,0:T(8,128)(2,1)S(1)} %copy.68), channel_id=1, replica_groups=mesh['blk'=128,'chan'=2] {'chan'}, dimensions={2}, use_global_device_ids=true | all-gather | bytes 884736 | tf_op jit(solution)/shard_map/all_gather | solution.py:146
  20.1 2.3 %reshape.57 = f32[64,6,514]{0,2,1:T(8,128)} reshape(f32[64,3,2,257,2]{0,4,3,2,1:T(2,128)S(1)} %copy.71) | data formatting | bytes 1579008 | tf_op jit(solution)/shard_map/reshape | solution.py:128
  27.2 2.0 %all_gather.22 = bf16[3,3,128,128]{3,2,1,0:T(8,128)(2,1)S(1)} all-gather(bf16[3,3,64,128]{3,2,1,0:T(8,128)(2,1)S(1)} %copy-done), channel_id=1, replica_groups=mesh['blk'=128,'chan'=2] {'chan'}, dimensions={2}, use_global_device_ids=true | all-gather | bytes 442368 | tf_op jit(solution)/shard_map/all_gather | solution.py:146
  35.5 2.6 %all_gather.26 = bf16[128,7,512]{2,0,1:T(8,128)(2,1)S(1)} all-gather(bf16[64,7,512]{2,0,1:T(8,128)(2,1)S(1)} %get-tuple-element.41), channel_id=1, replica_groups=mesh['blk'=128,'chan'=2] {'chan'}, dimensions={0}, use_global_device_ids=true | all-gather | bytes 1376256 | tf_op jit(solution)/shard_map/all_gather | solution.py:195
  41.5 2.3 %all_gather.27 = bf16[128,5,512]{2,0,1:T(8,128)(2,1)S(1)} all-gather(bf16[64,5,512]{2,0,1:T(8,128)(2,1)S(1)} %get-tuple-element.47), channel_id=1, replica_groups=mesh['blk'=128,'chan'=2] {'chan'}, dimensions={0}, use_global_device_ids=true | all-gather | bytes 983040 | tf_op jit(solution)/shard_map/all_gather | solution.py:200
  47.7 4.2 %all_to_all.25 = bf16[2,64,4,512]{3,1,2,0:T(8,128)(2,1)S(1)} all-to-all(bf16[2,64,4,512]{3,1,2,0:T(8,128)(2,1)S(1)} %pad_maximum_fusion.6), channel_id=1, replica_groups=mesh['blk'=128,'chan'=2] {'chan'}, dimensions={0} | all-to-all | bytes 1048576 | tf_op jit(solution)/shard_map/all_to_all | solution.py:11
  55.5 1.6 collective-permute-start.3
  57.1 2.6 %collective-permute-start.4 = (bf16[64,1,512]{2,0,1:T(8,128)(2,1)S(1)}, bf16[64,1,512]{2,0,1:T(8,128)(2,1)S(1)}, u32[]{:S(2)}, u32[]{:S(2)}) collective-permute-start(bf16[64,1,512]{2,0,1:T(8,128)(2,1)S(1)} %get-tuple-element.35), channel_id=1, source_target_pairs={{0,254},{2,0},{4,2},{6,4},{8,6},{10,8},{12,10},{14,12},{16,14},{18... | collective-permute-start | bytes 196616 | tf_op jit(solution)/shard_map/ppermute | solution.py:30
  61.5 1.5 fusion.103
  64.8 1.5 fusion.105
  67.1 3.5 %all-to-all-start.1 = ((bf16[2,64,4,512]{3,1,2,0:T(8,128)(2,1)}), bf16[2,64,4,512]{3,1,2,0:T(8,128)(2,1)S(1)}, u32[]{:S(2)}, u32[]{:S(2)}) async-start(bf16[2,64,4,512]{3,1,2,0:T(8,128)(2,1)} %pad_maximum_fusion.8), calls=%async_computation.1 | async-start | bytes 1048576 | tf_op jit(solution)/shard_map/all_to_all | solution.py:11
  72.4 19.3 %all-to-all-start.2 = ((f32[128,1,2304]{2,1,0:T(1,128)}), f32[128,1,2304]{2,1,0:T(1,128)S(1)}, u32[]{:S(2)}, u32[]{:S(2)}) async-start(f32[128,1,2304]{2,1,0:T(1,128)} %bitcast.150), calls=%async_computation.2 | async-start | bytes 2359296 | tf_op jit(solution)/shard_map/all_to_all | solution.py:171
  91.7 2.0 %all_gather.21 = bf16[3,3,128,128]{3,2,1,0:T(8,128)(2,1)S(1)} all-gather(bf16[3,3,64,128]{3,2,1,0:T(8,128)(2,1)S(1)} %copy-done.1), channel_id=1, replica_groups=mesh['blk'=128,'chan'=2] {'chan'}, dimensions={2}, use_global_device_ids=true | all-gather | bytes 442368 | tf_op jit(solution)/shard_map/all_gather | solution.py:146
  94.9 30.9 %all-to-all-done.2 = f32[128,1,2304]{2,1,0:T(1,128)S(1)} async-done(((f32[128,1,2304]{2,1,0:T(1,128)}), f32[128,1,2304]{2,1,0:T(1,128)S(1)}, u32[]{:S(2)}, u32[]{:S(2)}) %all-to-all-start.2) | async-done | bytes 1179680 | tf_op jit(solution)/shard_map/all_to_all | solution.py:171
  126.5 1.6 broadcast_in_dim.2
  128.1 6.3 %all-to-all-start.3 = ((f32[128,1,2304]{2,1,0:T(1,128)}), f32[128,1,2304]{2,1,0:T(1,128)S(1)}, u32[]{:S(2)}, u32[]{:S(2)}) async-start(f32[128,1,2304]{2,1,0:T(1,128)} %broadcast_in_dim.2), calls=%async_computation.3 | async-start | bytes 2359296 | tf_op jit(solution)/shard_map/all_to_all | solution.py:174
  136.9 1.8 %collective-permute-start.5 = (bf16[64,1,512]{2,0,1:T(8,128)(2,1)S(1)}, bf16[64,1,512]{2,0,1:T(8,128)(2,1)S(1)}, u32[]{:S(2)}, u32[]{:S(2)}) collective-permute-start(bf16[64,1,512]{2,0,1:T(8,128)(2,1)S(1)} %get-tuple-element.32), channel_id=1, source_target_pairs={{0,2},{2,4},{4,6},{6,8},{8,10},{10,12},{12,14},{14,16},{16,18},{18... | collective-permute-start | bytes 196616 | tf_op jit(solution)/shard_map/ppermute | solution.py:30
  138.7 2.7 %collective-permute-start.6 = (bf16[64,1,512]{2,0,1:T(8,128)(2,1)S(1)}, bf16[64,1,512]{2,0,1:T(8,128)(2,1)S(1)}, u32[]{:S(2)}, u32[]{:S(2)}) collective-permute-start(bf16[64,1,512]{2,0,1:T(8,128)(2,1)S(1)} %get-tuple-element.33), channel_id=1, source_target_pairs={{0,254},{2,0},{4,2},{6,4},{8,6},{10,8},{12,10},{14,12},{16,14},{18... | collective-permute-start | bytes 196616 | tf_op jit(solution)/shard_map/ppermute | solution.py:30
  141.4 3.5 %collective-permute-done.5 = bf16[64,1,512]{2,0,1:T(8,128)(2,1)S(1)} collective-permute-done((bf16[64,1,512]{2,0,1:T(8,128)(2,1)S(1)}, bf16[64,1,512]{2,0,1:T(8,128)(2,1)S(1)}, u32[]{:S(2)}, u32[]{:S(2)}) %collective-permute-start.5) | collective-permute-done | bytes 65568 | tf_op jit(solution)/shard_map/ppermute | solution.py:30
  146.4 21.3 %all-to-all-done.3 = f32[128,1,2304]{2,1,0:T(1,128)S(1)} async-done(((f32[128,1,2304]{2,1,0:T(1,128)}), f32[128,1,2304]{2,1,0:T(1,128)S(1)}, u32[]{:S(2)}, u32[]{:S(2)}) %all-to-all-start.3) | async-done | bytes 1179680 | tf_op jit(solution)/shard_map/all_to_all | solution.py:174
  (135 shorter events, 44.1 us)
Async XLA Ops:
  2.8 9.0 %copy-start.3 = (bf16[128,2,256]{2,1,0:T(2,128)(2,1)S(1)}, bf16[128,2,256]{2,1,0:T(2,128)(2,1)}, u32[]{:S(2)}) copy-start(bf16[128,2,256]{2,1,0:T(2,128)(2,1)} %param.10) | copy-start | bytes 393220
  3.9 10.3 %copy-start.2 = (bf16[3,3,128,128]{3,2,1,0:T(8,128)(2,1)S(1)}, bf16[3,3,128,128]{3,2,1,0:T(8,128)(2,1)}, u32[]{:S(2)}) copy-start(bf16[3,3,128,128]{3,2,1,0:T(8,128)(2,1)} %param.9) | copy-start | bytes 884740
  7.0 22.3 %collective-permute-start.1 = (bf16[128,3,512]{2,0,1:T(8,128)(2,1)}, bf16[128,3,512]{2,0,1:T(8,128)(2,1)}, u32[]{:S(2)}, u32[]{:S(2)}) collective-permute-start(bf16[128,3,512]{2,0,1:T(8,128)(2,1)} %slice.569), channel_id=1, source_target_pairs={{0,2},{2,4},{4,6},{6,8},{8,10},{10,12},{12,14},{14,16},{16,18},{18... | collective-permute-start | bytes 1179656 | tf_op jit(solution)/shard_map/ppermute | solution.py:47
  9.2 21.2 %collective-permute-start.2 = (bf16[128,2,512]{2,0,1:T(8,128)(2,1)}, bf16[128,2,512]{2,0,1:T(8,128)(2,1)}, u32[]{:S(2)}, u32[]{:S(2)}) collective-permute-start(bf16[128,2,512]{2,0,1:T(8,128)(2,1)} %slice.570), channel_id=1, source_target_pairs={{2,0},{4,2},{6,4},{8,6},{10,8},{12,10},{14,12},{16,14},{18,16},{20... | collective-permute-start | bytes 786440 | tf_op jit(solution)/shard_map/ppermute | solution.py:48
  23.5 5.7 %collective-permute-start = (bf16[64,1,512]{2,0,1:T(8,128)(2,1)S(1)}, bf16[64,1,512]{2,0,1:T(8,128)(2,1)S(1)}, u32[]{:S(2)}, u32[]{:S(2)}) collective-permute-start(bf16[64,1,512]{2,0,1:T(8,128)(2,1)S(1)} %copy.112), channel_id=1, source_target_pairs={{0,254},{2,0},{4,2},{6,4},{8,6},{10,8},{12,10},{14,12},{16,14},{18... | collective-permute-start | bytes 196616 | tf_op jit(solution)/shard_map/ppermute | solution.py:30
  26.3 0.9 copy-start
  30.3 1.2 copy-start.1
  55.5 8.8 %collective-permute-start.3 = (bf16[64,1,512]{2,0,1:T(8,128)(2,1)S(1)}, bf16[64,1,512]{2,0,1:T(8,128)(2,1)S(1)}, u32[]{:S(2)}, u32[]{:S(2)}) collective-permute-start(bf16[64,1,512]{2,0,1:T(8,128)(2,1)S(1)} %get-tuple-element.34), channel_id=1, source_target_pairs={{0,2},{2,4},{4,6},{6,8},{8,10},{10,12},{12,14},{14,16},{16,18},{18... | collective-permute-start | bytes 196616 | tf_op jit(solution)/shard_map/ppermute | solution.py:30
  57.1 7.3 %collective-permute-start.4 = (bf16[64,1,512]{2,0,1:T(8,128)(2,1)S(1)}, bf16[64,1,512]{2,0,1:T(8,128)(2,1)S(1)}, u32[]{:S(2)}, u32[]{:S(2)}) collective-permute-start(bf16[64,1,512]{2,0,1:T(8,128)(2,1)S(1)} %get-tuple-element.35), channel_id=1, source_target_pairs={{0,254},{2,0},{4,2},{6,4},{8,6},{10,8},{12,10},{14,12},{16,14},{18... | collective-permute-start | bytes 196616 | tf_op jit(solution)/shard_map/ppermute | solution.py:30
  67.1 5.2 %all-to-all-start.1 = ((bf16[2,64,4,512]{3,1,2,0:T(8,128)(2,1)}), bf16[2,64,4,512]{3,1,2,0:T(8,128)(2,1)S(1)}, u32[]{:S(2)}, u32[]{:S(2)}) async-start(bf16[2,64,4,512]{3,1,2,0:T(8,128)(2,1)} %pad_maximum_fusion.8), calls=%async_computation.1 | async-start | bytes 1048576 | tf_op jit(solution)/shard_map/all_to_all | solution.py:11
  72.4 53.4 %all-to-all-start.2 = ((f32[128,1,2304]{2,1,0:T(1,128)}), f32[128,1,2304]{2,1,0:T(1,128)S(1)}, u32[]{:S(2)}, u32[]{:S(2)}) async-start(f32[128,1,2304]{2,1,0:T(1,128)} %bitcast.150), calls=%async_computation.2 | async-start | bytes 2359296 | tf_op jit(solution)/shard_map/all_to_all | solution.py:171
  128.1 39.6 %all-to-all-start.3 = ((f32[128,1,2304]{2,1,0:T(1,128)}), f32[128,1,2304]{2,1,0:T(1,128)S(1)}, u32[]{:S(2)}, u32[]{:S(2)}) async-start(f32[128,1,2304]{2,1,0:T(1,128)} %broadcast_in_dim.2), calls=%async_computation.3 | async-start | bytes 2359296 | tf_op jit(solution)/shard_map/all_to_all | solution.py:174
  136.9 8.0 %collective-permute-start.5 = (bf16[64,1,512]{2,0,1:T(8,128)(2,1)S(1)}, bf16[64,1,512]{2,0,1:T(8,128)(2,1)S(1)}, u32[]{:S(2)}, u32[]{:S(2)}) collective-permute-start(bf16[64,1,512]{2,0,1:T(8,128)(2,1)S(1)} %get-tuple-element.32), channel_id=1, source_target_pairs={{0,2},{2,4},{4,6},{6,8},{8,10},{10,12},{12,14},{14,16},{16,18},{18... | collective-permute-start | bytes 196616 | tf_op jit(solution)/shard_map/ppermute | solution.py:30
  138.7 6.2 %collective-permute-start.6 = (bf16[64,1,512]{2,0,1:T(8,128)(2,1)S(1)}, bf16[64,1,512]{2,0,1:T(8,128)(2,1)S(1)}, u32[]{:S(2)}, u32[]{:S(2)}) collective-permute-start(bf16[64,1,512]{2,0,1:T(8,128)(2,1)S(1)} %get-tuple-element.33), channel_id=1, source_target_pairs={{0,254},{2,0},{4,2},{6,4},{8,6},{10,8},{12,10},{14,12},{16,14},{18... | collective-permute-start | bytes 196616 | tf_op jit(solution)/shard_map/ppermute | solution.py:30
